TPU v7x, 512 devices: a whole 4x8x8 slice. The times are simulated.
512 devices in a mesh: depth: 16 (over y, core), lat: 32 (over x, z).
Axes of the slice: x: 4, y: 8, z: 8, core: 2. Of those that a mesh axis runs over, the one named last changes fastest.
Arguments:
- slices: float32 [48, 2, 256, 8192], P('depth', None, None, 'lat'), may hold values from -1.23 to 1.23, as said below
- section_counts: int32 [16], P('depth'), may hold values from 1 to 3, as said below
- scan_rows: int32 [256], P('lat'), may hold values from 0 to 128, as said below
- scan_columns: int32 [256], P('lat'), may hold values from 0 to 256, as said below
- tick_order: int32 [32, 8], P('lat'), may hold values from 0 to 7, each once within a row
- measured: float32 [256, 128, 128], P('lat'), may hold values from 0.2 to 2
- illumination: float32 [2, 128, 128], replicated, may hold values from -4.2 to 4.2
Outputs:
- slice_grad: float32 [48, 2, 256, 8192], P('depth', None, None, 'lat')
- position_loss: float32 [32, 8], P('lat')
Inputs may be any that keep to these rules, and one draw needn't show every extreme that they name: `slices`: the real and imaginary parts of transmission values of magnitude near one. `section_counts`: some section uses all 3 slots and some other section uses one. `scan_rows`: both ends are reached in every draw. `scan_columns`: a window may reach up to 128 columns into the next tile, the last tile continuing into the first; both ends are reached in every draw. `tick_order`: each row lists the tile's 8 positions once.
All inputs are finite; a program needn't handle non-finite values.
Results may differ from a plain program's by a relative error of at most 0.0003.
Values sent between devices are 32-bit elements; how exact they have to be, the bound alone decides.
No kernel may reach another device: no remote copies, remote signals or barrier semaphores. Data moves between devices by JAX's collectives and lax.ppermute only.
A program may use at most 128 MiB of HBM per device.

v0:
```python
import functools

import jax
import jax.numpy as jnp
import numpy as np
from jax import lax
from jax.experimental import pallas as pl
from jax.experimental.pallas import tpu as pltpu
from jax.sharding import PartitionSpec as P


FRESNEL = 12.0
W = 128
f32 = jnp.float32
bf16 = jnp.bfloat16
ORDER = 16
COUNT = 24
PLACE = 25


def moved(block, axis, distance):
    count = lax.axis_size(axis)
    return lax.ppermute(block, axis, [((i - distance) % count, i) for i in range(count)])


def swapped(block):
    count = lax.axis_size("depth")
    return lax.ppermute(block, "depth", [(i ^ 1, i) for i in range(count)])


def three_parts(array):
    parts = []
    rest = np.asarray(array, np.float64)
    for _ in range(3):
        part = rest.astype(np.float32).astype(bf16)
        parts.append(part)
        rest = rest - part.astype(np.float64)
    return parts


def right_table(matrix):
    first, second, third = three_parts(np.concatenate([matrix.real, matrix.imag], 1))
    return np.concatenate([first, first, second, third], 0)


def left_table(matrix):
    first, second, third = three_parts(np.concatenate([matrix.real, matrix.imag], 0))
    return np.concatenate(
        [np.concatenate([first, first], 1), np.concatenate([second, third], 1)], 0
    )


def make_tables(width):
    index = np.arange(width)
    fourier = np.exp(-2j * np.pi * (np.outer(index, index) % width) / width) / np.sqrt(width)
    frequency = ((index + width // 2) % width - width // 2) / width
    chirp = np.exp(-1j * FRESNEL * frequency * frequency)
    step = np.conj(fourier) @ (chirp[:, None] * fourier)
    return tuple(make(matrix) for matrix in (step, fourier) for make in (right_table, left_table))


def halves(value):
    high = value.astype(bf16)
    return high, (value - high.astype(f32)).astype(bf16)


def product(a, b):
    return jnp.dot(a, b, preferred_element_type=f32)


def spread_out(part, right):
    high, low = halves(part)
    return product(jnp.concatenate([high, low, high, high], 1), right)


def combined(z, conjugate):
    if conjugate:
        return jnp.concatenate([z[0][:, :W] + z[1][:, W:], z[1][:, :W] - z[0][:, W:]], 1)
    return jnp.concatenate([z[0][:, :W] - z[1][:, W:], z[0][:, W:] + z[1][:, :W]], 1)


def two_sided(real, imag, right, left, conjugate):
    y = combined([spread_out(part, right) for part in (real, imag)], conjugate)
    high, low = halves(y)
    z = product(left[: 2 * W], jnp.concatenate([high, low], 0)) + product(
        left[2 * W :], jnp.concatenate([high, high], 0)
    )
    if conjugate:
        return z[:W, :W] + z[W:, W:], z[:W, W:] - z[W:, :W]
    return z[:W, :W] - z[W:, W:], z[:W, W:] + z[W:, :W]


def at_window(meta, p, tile):
    positions = 8
    row = pl.multiple_of(jnp.minimum(meta[p] // 8 * 8, tile - W - 8), 8)
    block = jnp.minimum(meta[positions + p] // W, tile // W - 1)
    start = pl.multiple_of(block * W, W)
    after = pl.multiple_of(block * W + W, W)
    return row, meta[p] - row, start, after, meta[positions + p] - block * W


def cut_kernel(meta, own, rim, out, extended, *, base):
    slots = rim.shape[0]
    positions = out.shape[0]
    tile = own.shape[3]
    for slot in range(slots):
        for part in range(2):
            extended[2 * slot + part, :, :tile] = own[base + slot, part]
            extended[2 * slot + part, :, tile:] = rim[slot, part]
    lane = lax.broadcasted_iota(jnp.int32, (W + 8, W), 1)
    stamp = jnp.full((8, W), meta[COUNT], jnp.int32).astype(f32)

    def one_position(p, carry):
        row, drop, start, after, shift = at_window(meta, p, tile)
        lift = (W + 8 - drop) % (W + 8)
        turn = (W - shift) % W
        for plane in range(2 * slots):
            first = extended[plane, pl.ds(row, W + 8), pl.ds(start, W)]
            second = extended[plane, pl.ds(row, W + 8), pl.ds(after, W)]
            both = jnp.where(
                lane < W - shift, pltpu.roll(first, turn, 1), pltpu.roll(second, turn, 1)
            )
            out[p, plane * W : (plane + 1) * W, :] = pltpu.roll(both, lift, 0)[:W]
        if base == 0:
            out[p, 2 * slots * W :, :] = stamp
        return carry

    lax.fori_loop(0, positions, one_position, 0)


def two_sided_each(fields, right, left, conjugate):
    every = [
        spread_out(jnp.concatenate([field[part] for field in fields], 0), right) for part in range(2)
    ]
    results = []
    for index in range(len(fields)):
        y = combined([z[index * W : index * W + W] for z in every], conjugate)
        high, low = halves(y)
        z = product(left[: 2 * W], jnp.concatenate([high, low], 0)) + product(
            left[2 * W :], jnp.concatenate([high, high], 0)
        )
        if conjugate:
            results.append((z[:W, :W] + z[W:, W:], z[:W, W:] - z[W:, :W]))
        else:
            results.append((z[:W, :W] - z[W:, W:], z[:W, W:] + z[W:, :W]))
    return results


def times(a, b):
    return a[0] * b[0] - a[1] * b[1], a[0] * b[1] + a[1] * b[0]


def times_conjugate(a, b):
    return a[0] * b[0] + a[1] * b[1], a[0] * b[1] - a[1] * b[0]


def wave_kernel(
    meta,
    mine_zero,
    other_zero,
    mine_rest,
    other_rest,
    measured,
    illumination,
    step_right,
    step_left,
    far_right,
    far_left,
    out,
    counts,
):
    chips = mine_zero.shape[0]
    sections = 2 * chips
    core = meta[PLACE] % 2
    for chip in range(chips):
        own = jnp.max(mine_zero[chip, 2 * W :, :]).astype(jnp.int32)
        its = jnp.max(other_zero[chip, 2 * W :, :]).astype(jnp.int32)
        counts[2 * chip] = jnp.where(core == 0, own, its)
        counts[2 * chip + 1] = jnp.where(core == 0, its, own)

    def zero_window(section):
        chip = section // 2
        local = section % 2 == core
        return tuple(
            jnp.where(
                local,
                mine_zero[chip, part * W : part * W + W, :],
                other_zero[chip, part * W : part * W + W, :],
            )
            for part in range(2)
        )

    def rest_window(section, slot):
        chip = section // 2
        local = section % 2 == core
        at = pl.multiple_of((slot - 1) * 2 * W, 2 * W)
        return tuple(
            jnp.where(
                local,
                mine_rest[chip, pl.ds(at + part * W, W), :],
                other_rest[chip, pl.ds(at + part * W, W), :],
            )
            for part in range(2)
        )

    def any_window(section, slot):
        pairs = zip(zero_window(section), rest_window(section, jnp.maximum(slot, 1)))
        return tuple(jnp.where(slot == 0, a, b) for a, b in pairs)

    def keep(chip, field):
        out[chip, :W, :] = field[0]
        out[chip, W : 2 * W, :] = field[1]

    def ahead(field, window):
        return two_sided(*times(field, window), step_right[...], step_left[...], False)

    def back(field, window):
        return times_conjugate(window, two_sided(*field, step_right[...], step_left[...], True))

    def forward_section(section, field):
        @pl.when((core == 0) & (section % 2 == 0))
        def _():
            keep(section // 2, field)

        field = ahead(field, zero_window(section))
        return lax.fori_loop(
            1, counts[section], lambda slot, value: ahead(value, rest_window(section, slot)), field
        )

    def backward_section(index, field):
        section = sections - 2 - index

        @pl.when(section % 2 == 1)
        def _():
            keep(section // 2, field)

        count = counts[section]
        field = lax.fori_loop(
            1, count, lambda step, value: back(value, rest_window(section, count - step)), field
        )
        return back(field, zero_window(section))

    last = sections - 1
    final = counts[last] - 1
    field = lax.fori_loop(0, last, forward_section, (illumination[0], illumination[1]))
    field = lax.fori_loop(
        0, final, lambda slot, value: ahead(value, any_window(last, slot)), field
    )
    field = times(field, any_window(last, final))
    real, imag = two_sided(*field, far_right[...], far_left[...], False)
    misfit = real * real + imag * imag - measured[meta[PLACE] // 2]
    loss = jnp.sum(misfit * misfit) * (1.0 / (W * W))
    for chip in range(chips):
        out[chip, 2 * W :, :] = jnp.full((8, W), loss, f32)

    @pl.when(core == 1)
    def _():
        spread = two_sided(
            4.0 * misfit * real, 4.0 * misfit * imag, far_right[...], far_left[...], True
        )
        keep(chips - 1, spread)
        value = times_conjugate(any_window(last, final), spread)
        value = lax.fori_loop(
            0, final, lambda step, value: back(value, any_window(last, final - 1 - step)), value
        )
        keep(0, lax.fori_loop(0, sections - 3, backward_section, value))


GROUP = 4


def fields_of(ref, group, at):
    return [
        tuple(ref[group * GROUP + each, pl.ds(at + part * W, W), :] for part in range(2))
        for each in range(GROUP)
    ]


def put_fields(ref, group, at, fields):
    for each in range(GROUP):
        for part in range(2):
            ref[group * GROUP + each, pl.ds(at + part * W, W), :] = fields[each][part]


def window_of(zero, rest, group, slot):
    at = pl.multiple_of(jnp.maximum(slot - 1, 0) * 2 * W, 2 * W)
    return [
        tuple(jnp.where(slot == 0, a, b) for a, b in zip(*pair))
        for pair in zip(fields_of(zero, group, 0), fields_of(rest, group, at))
    ]


def first_kernel(meta, zero, rest, arrived, step_right, step_left, track, handed):
    core = meta[PLACE] % 2
    top = meta[COUNT]
    groups = zero.shape[0] // GROUP
    sections = 2 * zero.shape[0]

    @pl.when(core == 0)
    def _():
        def one_group(group, carry):
            put_fields(handed, group, 0, fields_of(arrived, group, 0))

            def one(slot, inner):
                at = pl.multiple_of(slot * 2 * W, 2 * W)
                fields = fields_of(handed, group, 0)
                put_fields(track, group, at, fields)
                cut = window_of(zero, rest, group, slot)
                fields = [times(a, b) for a, b in zip(fields, cut)]
                put_fields(
                    handed, group, 0, two_sided_each(fields, step_right[...], step_left[...], False)
                )
                return inner

            return lax.fori_loop(0, top, one, carry)

        lax.fori_loop(0, groups, one_group, 0)

    @pl.when(core == 1)
    def _():
        def one_group(group, carry):
            put_fields(handed, group, 0, fields_of(arrived, group, 0))

            def one(step, inner):
                at = pl.multiple_of((top - 1 - step) * 2 * W, 2 * W)
                fields = fields_of(handed, group, 0)
                spread = two_sided_each(fields, step_right[...], step_left[...], True)
                done = (step == 0) & (meta[PLACE] == sections - 1)
                spread = [
                    tuple(jnp.where(done, kept, fresh) for kept, fresh in zip(a, b))
                    for a, b in zip(fields, spread)
                ]
                put_fields(track, group, at, spread)
                cut = window_of(zero, rest, group, top - 1 - step)
                put_fields(handed, group, 0, [times_conjugate(a, b) for a, b in zip(cut, spread)])
                return inner

            return lax.fori_loop(0, top, one, carry)

        lax.fori_loop(0, groups, one_group, 0)


def second_kernel(
    meta, zero, rest, track, handed, arrived, step_right, step_left, main, rim, losses, pulls, state, total
):
    core = meta[PLACE] % 2
    top = meta[COUNT]
    groups = zero.shape[0] // GROUP

    @pl.when(core == 0)
    def _():
        def one_group(group, carry):
            put_fields(state, group, 0, fields_of(handed, group, 0))

            def one(step, inner):
                at = pl.multiple_of((top - 1 - step) * 2 * W, 2 * W)
                fields = fields_of(state, group, 0)
                spread = two_sided_each(fields, step_right[...], step_left[...], True)
                waves = fields_of(track, group, at)
                put_fields(pulls, group, at, [times_conjugate(a, b) for a, b in zip(waves, spread)])
                cut = window_of(zero, rest, group, top - 1 - step)
                put_fields(state, group, 0, [times_conjugate(a, b) for a, b in zip(cut, spread)])
                return inner

            return lax.fori_loop(0, top, one, carry)

        lax.fori_loop(0, groups, one_group, 0)

    @pl.when(core == 1)
    def _():
        def one_group(group, carry):
            put_fields(state, group, 0, fields_of(handed, group, 0))

            def pull(slot):
                at = pl.multiple_of(slot * 2 * W, 2 * W)
                fields = fields_of(state, group, 0)
                spread = fields_of(track, group, at)
                put_fields(pulls, group, at, [times_conjugate(a, b) for a, b in zip(fields, spread)])
                return fields

            def one(slot, inner):
                fields = pull(slot)
                cut = window_of(zero, rest, group, slot)
                fields = [times(a, b) for a, b in zip(fields, cut)]
                put_fields(
                    state, group, 0, two_sided_each(fields, step_right[...], step_left[...], False)
                )
                return inner

            lax.fori_loop(0, top - 1, one, carry)
            pull(top - 1)
            return carry

        lax.fori_loop(0, groups, one_group, 0)

    deposit(meta, pulls, arrived, main, rim, losses, total)


def deposit(meta, pulls, arrived, main, rim, losses, total):
    positions = pulls.shape[0]
    planes = pulls.shape[1] // W
    tile = main.shape[3]
    total[...] = jnp.zeros_like(total)
    lane = lax.broadcasted_iota(jnp.int32, (W + 8, W), 1)
    spare = jnp.zeros((8, W), f32)

    def one_position(p, carry):
        row, drop, start, after, shift = at_window(meta, p, tile)

        def one_slot(slot, inner):
            for part in range(2):
                at = pl.multiple_of((2 * slot + part) * W, W)
                pull = jnp.concatenate([pulls[p, pl.ds(at, W), :], spare], 0)
                pull = pltpu.roll(pltpu.roll(pull, drop, 0), shift % W, 1)
                plane = 2 * slot + part
                total[plane, pl.ds(row, W + 8), pl.ds(start, W)] += jnp.where(lane >= shift, pull, 0.0)
                total[plane, pl.ds(row, W + 8), pl.ds(after, W)] += jnp.where(lane < shift, pull, 0.0)
            return inner

        return lax.fori_loop(0, meta[COUNT], one_slot, carry)

    lax.fori_loop(0, positions, one_position, 0)
    for plane in range(planes):
        main[plane // 2, plane % 2] = total[plane, :, :tile]
        rim[plane // 2, plane % 2] = total[plane, :, tile:]
    place = lax.broadcasted_iota(jnp.int32, (1, W), 1)
    line = jnp.zeros((1, W), f32)
    for j in range(positions):
        line = jnp.where(place == j, arrived[meta[ORDER + j], 2 * W : 2 * W + 1, :], line)
    losses[...] = line[:, :positions]


def merge_kernel(main, rim, out):
    out[:, :, :, W:] = main[:, :, :, W:]
    out[:, :, :, :W] = main[:, :, :, :W] + rim[...]


VMEM = pl.BlockSpec(memory_space=pltpu.VMEM)
SMEM = pl.BlockSpec(memory_space=pltpu.SMEM)


def shards(slices, section_counts, scan_rows, scan_columns, tick_order, measured, illumination):
    slots = slices.shape[0]
    tile = slices.shape[3]
    positions = scan_rows.shape[0]
    planes = 2 * slots
    chips = lax.axis_size("depth") // 2
    place = lax.axis_index("depth")
    groups = [[2 * chip + core for chip in range(chips)] for core in range(2)]
    exchange = functools.partial(
        lax.all_to_all, axis_name="depth", split_axis=0, concat_axis=0, tiled=True, axis_index_groups=groups
    )
    params = pltpu.CompilerParams(vmem_limit_bytes=24 << 20)
    tables = [jnp.asarray(table) for table in make_tables(W)]
    meta = jnp.concatenate(
        [scan_rows, scan_columns, tick_order[0], section_counts, place.reshape(1)]
    ).astype(jnp.int32)

    def cut(base, count, rim):
        return pl.pallas_call(
            functools.partial(cut_kernel, base=base),
            out_shape=jax.ShapeDtypeStruct(
                (positions, 2 * count * W + (8 if base == 0 else 0), W), f32
            ),
            in_specs=[SMEM] + [VMEM] * 2,
            out_specs=VMEM,
            scratch_shapes=[pltpu.VMEM((2 * count, tile, tile + W), f32)],
            compiler_params=params,
            name="cut",
        )(meta, slices, rim)

    rim_zero = moved(slices[:1, ..., :W], "lat", -1)
    zero = cut(0, 1, rim_zero)
    edge, zero = lax.optimization_barrier((slices[1:, ..., :W], zero))
    rim_rest = moved(edge, "lat", -1)
    mine_zero = exchange(zero)
    other_zero = swapped(mine_zero)
    rest = cut(1, slots - 1, rim_rest)
    sent, _ = lax.optimization_barrier((rest, mine_zero))
    mine_rest = exchange(sent)
    other_rest = swapped(mine_rest)
    boundary = pl.pallas_call(
        wave_kernel,
        out_shape=jax.ShapeDtypeStruct((chips, 2 * W + 8, W), f32),
        in_specs=[SMEM] + [VMEM] * 10,
        out_specs=VMEM,
        scratch_shapes=[pltpu.SMEM((2 * chips,), jnp.int32)],
        compiler_params=params,
        name="wave",
    )(meta, mine_zero, other_zero, mine_rest, other_rest, measured, illumination, *tables)
    arrived = exchange(boundary)
    track, handed = pl.pallas_call(
        first_kernel,
        out_shape=(
            jax.ShapeDtypeStruct((positions, planes * W, W), f32),
            jax.ShapeDtypeStruct((positions, 2 * W, W), f32),
        ),
        in_specs=[SMEM] + [VMEM] * 5,
        out_specs=(VMEM,) * 2,
        compiler_params=params,
        name="first",
    )(meta, zero, rest, arrived, *tables[:2])
    main, overflow, losses = pl.pallas_call(
        second_kernel,
        out_shape=(
            jax.ShapeDtypeStruct((slots, 2, tile, tile), f32),
            jax.ShapeDtypeStruct((slots, 2, tile, W), f32),
            jax.ShapeDtypeStruct((1, positions), f32),
        ),
        in_specs=[SMEM] + [VMEM] * 7,
        out_specs=(VMEM,) * 3,
        scratch_shapes=[
            pltpu.VMEM((positions, planes * W, W), f32),
            pltpu.VMEM((positions, 2 * W, W), f32),
            pltpu.VMEM((planes, tile, tile + W), f32),
        ],
        compiler_params=params,
        name="second",
    )(meta, zero, rest, track, swapped(handed), arrived, *tables[:2])
    incoming = moved(overflow, "lat", 1)
    slice_grad = pl.pallas_call(
        merge_kernel,
        out_shape=jax.ShapeDtypeStruct((slots, 2, tile, tile), f32),
        in_specs=[VMEM] * 2,
        out_specs=VMEM,
        compiler_params=params,
        name="merge",
    )(main, incoming)
    return slice_grad, losses


def solution(mesh):
    placed = (
        P("depth", None, None, "lat"),
        P("depth"),
        P("lat"),
        P("lat"),
        P("lat", None),
        P("lat", None, None),
        P(),
    )
    return jax.shard_map(
        shards,
        mesh=mesh,
        in_specs=placed,
        out_specs=(P("depth", None, None, "lat"), P("lat", None)),
        check_vma=False,
    )
```

profile of v0, /device:TPU:8, one launch (start us, length us, event | category | flops | bytes accessed | tf_op | source)
XLA Modules:
  0.0 218.6 jit_solution(14920524912185990634)
XLA Ops:
  0.6 0.0 copy-start
  0.6 0.0 copy-start.11
  0.7 0.0 copy-start.10
  0.7 0.0 copy-start.9
  0.7 1.1 slice.7
  1.8 13.1 %collective-permute-start = (f32[1,2,256,128]{3,2,1,0:T(8,128)S(1)}, f32[1,2,256,128]{3,2,1,0:T(8,128)S(1)}, u32[]{:S(2)}, u32[]{:S(2)}) collective-permute-start(f32[1,2,256,128]{3,2,1,0:T(8,128)S(1)} %slice.7), channel_id=1, source_target_pairs={{1,0},{2,1},{3,2},{4,3},{5,4},{6,5},{7,6},{8,7},{9,8},{10,9},{11,1... | collective-permute-start | bytes 786440 | tf_op jit(solution)/shard_map/ppermute | solution.py:23
  14.9 1.9 slice.6
  17.4 0.0 copy-done.11
  17.5 0.0 copy-done.10
  17.5 0.0 copy-done.9
  17.5 0.1 concatenate.3.meta
  17.6 2.9 %collective-permute-done.rim = f32[1,2,256,128]{3,2,1,0:T(8,128)S(1)} collective-permute-done((f32[1,2,256,128]{3,2,1,0:T(8,128)S(1)}, f32[1,2,256,128]{3,2,1,0:T(8,128)S(1)}, u32[]{:S(2)}, u32[]{:S(2)}) %collective-permute-start) | collective-permute-done | bytes 262176 | tf_op jit(solution)/shard_map/ppermute | solution.py:23
  20.4 0.0 copy-done
  20.5 2.9 %cut.2.zero = f32[8,264,128]{2,1,0:T(8,128)} custom-call(s32[26]{0:T(128)S(1)} %concatenate.3.meta, f32[3,2,256,256]{3,2,1,0:T(8,128)S(1)} %copy-done, f32[1,2,256,128]{3,2,1,0:T(8,128)S(1)} %collective-permute-done.rim), custom_call_target="tpu_custom_call" | custom-call | tf_op jit(solution)/shard_map/cut/pallas_call | solution.py:460
  23.4 0.0 copy-start.8
  23.4 7.7 %all-to-all-start = ((f32[8,264,128]{2,1,0:T(8,128)}), f32[8,264,128]{2,1,0:T(8,128)S(1)}, u32[]{:S(2)}, u32[]{:S(2)}) async-start(f32[8,264,128]{2,1,0:T(8,128)} %cut.2.zero), calls=%async_computation | async-start | bytes 2162688 | tf_op jit(solution)/shard_map/all_to_all | solution.py:476
  31.0 0.0 copy-done.8
  31.0 7.7 %collective-permute-start.1 = (f32[2,2,256,128]{3,2,1,0:T(8,128)S(1)}, f32[2,2,256,128]{3,2,1,0:T(8,128)S(1)}, u32[]{:S(2)}, u32[]{:S(2)}) collective-permute-start(f32[2,2,256,128]{3,2,1,0:T(8,128)S(1)} %copy-done.8), channel_id=1, source_target_pairs={{1,0},{2,1},{3,2},{4,3},{5,4},{6,5},{7,6},{8,7},{9,8},{10,9},{11,1... | collective-permute-start | bytes 1572872 | tf_op jit(solution)/shard_map/ppermute | solution.py:23
  38.8 9.7 %collective-permute-done.1.rim = f32[2,2,256,128]{3,2,1,0:T(8,128)S(1)} collective-permute-done((f32[2,2,256,128]{3,2,1,0:T(8,128)S(1)}, f32[2,2,256,128]{3,2,1,0:T(8,128)S(1)}, u32[]{:S(2)}, u32[]{:S(2)}) %collective-permute-start.1) | collective-permute-done | bytes 524320 | tf_op jit(solution)/shard_map/ppermute | solution.py:23
  48.5 0.0 copy-start.1
  48.5 1.4 copy-done.1
  49.9 2.6 %cut.3.rest = f32[8,512,128]{2,1,0:T(8,128)S(1)} custom-call(s32[26]{0:T(128)S(1)} %concatenate.3.meta, f32[3,2,256,256]{3,2,1,0:T(8,128)S(1)} %copy-done.1, f32[2,2,256,128]{3,2,1,0:T(8,128)S(1)} %collective-permute-done.1.rim), custom_call_target="tpu_custom_call" | custom-call | tf_op jit(solution)/shard_map/cut/pallas_call | solution.py:460
  52.5 0.0 copy-start.2
  52.5 5.7 %all-to-all-done.mine_zero = f32[8,264,128]{2,1,0:T(8,128)S(1)} async-done(((f32[8,264,128]{2,1,0:T(8,128)}), f32[8,264,128]{2,1,0:T(8,128)S(1)}, u32[]{:S(2)}, u32[]{:S(2)}) %all-to-all-start) | async-done | bytes 1081376 | tf_op jit(solution)/shard_map/all_to_all | solution.py:476
  58.2 0.0 copy-start.3
  58.2 0.0 copy-start.4
  58.2 0.0 copy-start.5
  58.2 0.0 copy-start.6
  58.2 0.0 copy-start.7
  58.2 54.2 %all_to_all.15.mine_rest = f32[8,512,128]{2,1,0:T(8,128)S(1)} all-to-all(f32[8,512,128]{2,1,0:T(8,128)S(1)} %cut.3.rest), channel_id=1, replica_groups={{0,64,128,192,256,320,384,448},{32,96,160,224,288,352,416,480},{1,65,12..., dimensions={0} | all-to-all | bytes 4194304 | tf_op jit(solution)/shard_map/all_to_all | solution.py:480
  112.4 1.9 collective-permute-start.3
  114.3 2.4 %collective-permute-start.2 = (f32[8,264,128]{2,1,0:T(8,128)S(1)}, f32[8,264,128]{2,1,0:T(8,128)S(1)}, u32[]{:S(2)}, u32[]{:S(2)}) collective-permute-start(f32[8,264,128]{2,1,0:T(8,128)S(1)} %all-to-all-done.mine_zero), channel_id=1, source_target_pairs={{32,0},{0,32},{96,64},{64,96},{160,128},{128,160},{224,192},{192,2... | collective-permute-start | bytes 3244040 | tf_op jit(solution)/shard_map/ppermute | solution.py:28
  116.8 3.3 %collective-permute-done.2.other_zero = f32[8,264,128]{2,1,0:T(8,128)S(1)} collective-permute-done((f32[8,264,128]{2,1,0:T(8,128)S(1)}, f32[8,264,128]{2,1,0:T(8,128)S(1)}, u32[]{:S(2)}, u32[]{:S(2)}) %collective-permute-start.2) | collective-permute-done | bytes 1081376 | tf_op jit(solution)/shard_map/ppermute | solution.py:28
  120.0 0.0 collective-permute-done.3.other_rest
  120.0 0.0 copy-done.2
  120.0 0.0 copy-done.3
  120.0 0.0 copy-done.4
  120.0 0.0 copy-done.5
  120.0 0.0 copy-done.6
  120.1 0.0 copy-done.7
  120.1 17.0 %wave.1 = f32[8,264,128]{2,1,0:T(8,128)S(1)} custom-call(s32[26]{0:T(128)S(1)} %concatenate.3.meta, f32[8,264,128]{2,1,0:T(8,128)S(1)} %all-to-all-done.mine_zero, f32[8,264,128]{2,1,0:T(8,128)S(1)} %collective-permute-done.2.other_zero, f32[8,512,128]{2,1,0:T(8,128)S(1)} %all_to_all.15.mine_rest, f32[8,512,128]{2,1,0:T(8,128)S(1)} %collective-permute-done.3.other_rest, ...), custom_call_target="tpu_custom_call" | custom-call | tf_op jit(solution)/shard_map/wave/pallas_call | solution.py:482
  137.0 21.6 %all_to_all.16.arrived = f32[8,264,128]{2,1,0:T(8,128)S(1)} all-to-all(f32[8,264,128]{2,1,0:T(8,128)S(1)} %wave.1), channel_id=1, replica_groups={{0,64,128,192,256,320,384,448},{32,96,160,224,288,352,416,480},{1,65,12..., dimensions={0} | all-to-all | bytes 2162688 | tf_op jit(solution)/shard_map/all_to_all | solution.py:491
  158.7 6.2 %first.1 = (f32[8,768,128]{2,1,0:T(8,128)S(1)}, f32[8,256,128]{2,1,0:T(8,128)S(1)}) custom-call(s32[26]{0:T(128)S(1)} %concatenate.3.meta, f32[8,264,128]{2,1,0:T(8,128)} %cut.2.zero, f32[8,512,128]{2,1,0:T(8,128)S(1)} %cut.3.rest, f32[8,264,128]{2,1,0:T(8,128)S(1)} %all_to_all.16.arrived, bf16[512,256]{1,0:T(8,128)(2,1)S(1)} %copy-done.3, ...), custom_call_target="tpu_custom_call" | custom-call | tf_op jit(solution)/shard_map/first/pallas_call | solution.py:492
  164.9 15.6 %collective-permute-start.4 = (f32[8,256,128]{2,1,0:T(8,128)S(1)}, f32[8,256,128]{2,1,0:T(8,128)S(1)}, u32[]{:S(2)}, u32[]{:S(2)}) collective-permute-start(f32[8,256,128]{2,1,0:T(8,128)S(1)} %get-tuple-element.14), channel_id=1, source_target_pairs={{32,0},{0,32},{96,64},{64,96},{160,128},{128,160},{224,192},{192,2... | collective-permute-start | bytes 3145736 | tf_op jit(solution)/shard_map/ppermute | solution.py:28
  180.5 2.3 %collective-permute-done.4.handed = f32[8,256,128]{2,1,0:T(8,128)S(1)} collective-permute-done((f32[8,256,128]{2,1,0:T(8,128)S(1)}, f32[8,256,128]{2,1,0:T(8,128)S(1)}, u32[]{:S(2)}, u32[]{:S(2)}) %collective-permute-start.4) | collective-permute-done | bytes 1048608 | tf_op jit(solution)/shard_map/ppermute | solution.py:28
  182.8 10.3 %second.1 = (f32[3,2,256,256]{3,2,1,0:T(8,128)S(1)}, f32[3,2,256,128]{3,2,1,0:T(8,128)S(1)}, f32[1,8]{1,0:T(1,128)}) custom-call(s32[26]{0:T(128)S(1)} %concatenate.3.meta, f32[8,264,128]{2,1,0:T(8,128)} %cut.2.zero, f32[8,512,128]{2,1,0:T(8,128)S(1)} %cut.3.rest, f32[8,768,128]{2,1,0:T(8,128)S(1)} %get-tuple-element.13.track, ...), custom_call_target="tpu_custom_call" | custom-call | tf_op jit(solution)/shard_map/second/pallas_call | solution.py:503
  193.1 1.9 collective-permute-start.5
  195.0 22.3 %collective-permute-done.5.rim = f32[3,2,256,128]{3,2,1,0:T(8,128)S(1)} collective-permute-done((f32[3,2,256,128]{3,2,1,0:T(8,128)S(1)}, f32[3,2,256,128]{3,2,1,0:T(8,128)S(1)}, u32[]{:S(2)}, u32[]{:S(2)}) %collective-permute-start.5) | collective-permute-done | bytes 786464 | tf_op jit(solution)/shard_map/ppermute | solution.py:23
  217.3 1.3 merge.1
Async XLA Ops:
  0.6 19.8 %copy-start = (f32[3,2,256,256]{3,2,1,0:T(8,128)S(1)}, f32[3,2,256,256]{3,2,1,0:T(8,128)}, u32[]{:S(2)}) copy-start(f32[3,2,256,256]{3,2,1,0:T(8,128)} %own.3) | copy-start | bytes 4718596
  0.6 16.8 %copy-start.11 = (s32[1,8]{1,0:T(1,128)S(1)}, s32[1,8]{1,0:T(1,128)}, u32[]{:S(2)}) copy-start(s32[1,8]{1,0:T(1,128)} %param.15) | copy-start | bytes 100
  0.7 16.8 %copy-start.10 = (s32[8]{0:T(128)S(1)}, s32[8]{0:T(128)}, u32[]{:S(2)}) copy-start(s32[8]{0:T(128)} %param.14) | copy-start | bytes 100
  0.7 16.8 %copy-start.9 = (s32[8]{0:T(128)S(1)}, s32[8]{0:T(128)}, u32[]{:S(2)}) copy-start(s32[8]{0:T(128)} %param.13) | copy-start | bytes 100
  1.8 18.7 %collective-permute-start = (f32[1,2,256,128]{3,2,1,0:T(8,128)S(1)}, f32[1,2,256,128]{3,2,1,0:T(8,128)S(1)}, u32[]{:S(2)}, u32[]{:S(2)}) collective-permute-start(f32[1,2,256,128]{3,2,1,0:T(8,128)S(1)} %slice.7), channel_id=1, source_target_pairs={{1,0},{2,1},{3,2},{4,3},{5,4},{6,5},{7,6},{8,7},{9,8},{10,9},{11,1... | collective-permute-start | bytes 786440 | tf_op jit(solution)/shard_map/ppermute | solution.py:23
  23.4 7.7 %copy-start.8 = (f32[2,2,256,128]{3,2,1,0:T(8,128)S(1)}, f32[2,2,256,128]{3,2,1,0:T(8,128)}, u32[]{:S(2)}) copy-start(f32[2,2,256,128]{3,2,1,0:T(8,128)} %slice.6) | copy-start | bytes 1572868
  23.4 34.8 %all-to-all-start = ((f32[8,264,128]{2,1,0:T(8,128)}), f32[8,264,128]{2,1,0:T(8,128)S(1)}, u32[]{:S(2)}, u32[]{:S(2)}) async-start(f32[8,264,128]{2,1,0:T(8,128)} %cut.2.zero), calls=%async_computation | async-start | bytes 2162688 | tf_op jit(solution)/shard_map/all_to_all | solution.py:476
  31.0 17.5 %collective-permute-start.1 = (f32[2,2,256,128]{3,2,1,0:T(8,128)S(1)}, f32[2,2,256,128]{3,2,1,0:T(8,128)S(1)}, u32[]{:S(2)}, u32[]{:S(2)}) collective-permute-start(f32[2,2,256,128]{3,2,1,0:T(8,128)S(1)} %copy-done.8), channel_id=1, source_target_pairs={{1,0},{2,1},{3,2},{4,3},{5,4},{6,5},{7,6},{8,7},{9,8},{10,9},{11,1... | collective-permute-start | bytes 1572872 | tf_op jit(solution)/shard_map/ppermute | solution.py:23
  48.5 1.4 copy-start.1
  52.5 67.6 %copy-start.2 = (bf16[512,256]{1,0:T(8,128)(2,1)S(1)}, bf16[512,256]{1,0:T(8,128)(2,1)}, u32[]{:S(2)}) copy-start(bf16[512,256]{1,0:T(8,128)(2,1)} %constant.15.clone.step_left) | copy-start | bytes 786436
  58.2 61.9 %copy-start.3 = (bf16[512,256]{1,0:T(8,128)(2,1)S(1)}, bf16[512,256]{1,0:T(8,128)(2,1)}, u32[]{:S(2)}) copy-start(bf16[512,256]{1,0:T(8,128)(2,1)} %constant.14.clone.step_right) | copy-start | bytes 786436
  58.2 61.9 %copy-start.4 = (f32[8,128,128]{2,1,0:T(8,128)S(1)}, f32[8,128,128]{2,1,0:T(8,128)}, u32[]{:S(2)}) copy-start(f32[8,128,128]{2,1,0:T(8,128)} %measured.1) | copy-start | bytes 1572868
  58.2 61.9 %copy-start.5 = (bf16[512,256]{1,0:T(8,128)(2,1)S(1)}, bf16[512,256]{1,0:T(8,128)(2,1)}, u32[]{:S(2)}) copy-start(bf16[512,256]{1,0:T(8,128)(2,1)} %constant.17.clone.far_left) | copy-start | bytes 786436
  58.2 61.9 %copy-start.6 = (bf16[512,256]{1,0:T(8,128)(2,1)S(1)}, bf16[512,256]{1,0:T(8,128)(2,1)}, u32[]{:S(2)}) copy-start(bf16[512,256]{1,0:T(8,128)(2,1)} %constant.16.clone.far_right) | copy-start | bytes 786436
  58.2 61.9 %copy-start.7 = (f32[2,128,128]{2,1,0:T(8,128)S(1)}, f32[2,128,128]{2,1,0:T(8,128)}, u32[]{:S(2)}) copy-start(f32[2,128,128]{2,1,0:T(8,128)} %illumination.1) | copy-start | bytes 393220
  112.4 7.6 %collective-permute-start.3 = (f32[8,512,128]{2,1,0:T(8,128)S(1)}, f32[8,512,128]{2,1,0:T(8,128)S(1)}, u32[]{:S(2)}, u32[]{:S(2)}) collective-permute-start(f32[8,512,128]{2,1,0:T(8,128)S(1)} %all_to_all.15.mine_rest), channel_id=1, source_target_pairs={{32,0},{0,32},{96,64},{64,96},{160,128},{128,160},{224,192},{192,2... | collective-permute-start | bytes 6291464 | tf_op jit(solution)/shard_map/ppermute | solution.py:28
  114.3 5.7 %collective-permute-start.2 = (f32[8,264,128]{2,1,0:T(8,128)S(1)}, f32[8,264,128]{2,1,0:T(8,128)S(1)}, u32[]{:S(2)}, u32[]{:S(2)}) collective-permute-start(f32[8,264,128]{2,1,0:T(8,128)S(1)} %all-to-all-done.mine_zero), channel_id=1, source_target_pairs={{32,0},{0,32},{96,64},{64,96},{160,128},{128,160},{224,192},{192,2... | collective-permute-start | bytes 3244040 | tf_op jit(solution)/shard_map/ppermute | solution.py:28
  164.9 17.9 %collective-permute-start.4 = (f32[8,256,128]{2,1,0:T(8,128)S(1)}, f32[8,256,128]{2,1,0:T(8,128)S(1)}, u32[]{:S(2)}, u32[]{:S(2)}) collective-permute-start(f32[8,256,128]{2,1,0:T(8,128)S(1)} %get-tuple-element.14), channel_id=1, source_target_pairs={{32,0},{0,32},{96,64},{64,96},{160,128},{128,160},{224,192},{192,2... | collective-permute-start | bytes 3145736 | tf_op jit(solution)/shard_map/ppermute | solution.py:28
  193.1 24.3 %collective-permute-start.5 = (f32[3,2,256,128]{3,2,1,0:T(8,128)S(1)}, f32[3,2,256,128]{3,2,1,0:T(8,128)S(1)}, u32[]{:S(2)}, u32[]{:S(2)}) collective-permute-start(f32[3,2,256,128]{3,2,1,0:T(8,128)S(1)} %get-tuple-element.16), channel_id=1, source_target_pairs={{31,0},{0,1},{1,2},{2,3},{3,4},{4,5},{5,6},{6,7},{7,8},{8,9},{9,10... | collective-permute-start | bytes 2359304 | tf_op jit(solution)/shard_map/ppermute | solution.py:23
where the time goes:
time: 219 us
  blocking collectives  75.9 us (35%)
  starting transfers between devices  50.4 us (23%)
  waiting for transfers between devices  46.2 us (21%)
  Pallas kernels  40.2 us (18%)
  local copies, waits for them, and re-layouts  4.51 us (2%)
    all_to_all x1, blocking collectives, shards(): mine_rest = exchange(sent)  54.2 us
    ppermute x3, waiting for transfers between devices, moved(): lax.ppermute(block, axis, [((i - distance) % count, i) for i in range(cou...  35 us
    ppermute x3, starting transfers between devices, moved(): lax.ppermute(block, axis, [((i - distance) % count, i) for i in range(cou...  22.7 us
    all_to_all x1, blocking collectives, shards(): arrived = exchange(boundary)  21.6 us
    ppermute x3, starting transfers between devices, swapped(): return lax.ppermute(block, 'depth', [(i ^ 1, i) for i in range(count)])  20 us
    pallas_call x1, Pallas kernels, shards(): pl.pallas_call(wave_kernel, out_shape=jax.ShapeDtypeStruct((chips, 2 * W...  17 us
    pallas_call x1, Pallas kernels, shards(): pl.pallas_call(second_kernel, out_shape=(jax.ShapeDtypeStruct((slots, 2,...  10.3 us
    all_to_all x1, starting transfers between devices, shards(): mine_zero = exchange(zero)  7.68 us
  transfers between devices with their start and end apart: 7, of which 6 were waited for; matrix products, arithmetic and copies ran while one was open for 1% of the time, Pallas kernels for 1%

commit v1 on v0

--- a/solution.py
+++ b/solution.py
@@ -79,15 +79,28 @@
     return jnp.concatenate([z[0][:, :W] - z[1][:, W:], z[0][:, W:] + z[1][:, :W]], 1)
 
 
-def two_sided(real, imag, right, left, conjugate):
-    y = combined([spread_out(part, right) for part in (real, imag)], conjugate)
+def right_of(field, right, conjugate):
+    z = []
+    for part in field:
+        high, low = halves(part)
+        z.append(
+            product(jnp.concatenate([high, low], 1), right[: 2 * W])
+            + product(jnp.concatenate([high, high], 1), right[2 * W :])
+        )
+    return combined(z, conjugate)
+
+
+def left_of(y, left, conjugate):
     high, low = halves(y)
-    z = product(left[: 2 * W], jnp.concatenate([high, low], 0)) + product(
-        left[2 * W :], jnp.concatenate([high, high], 0)
+    first = jnp.concatenate([high, low], 0)
+    second = jnp.concatenate([high, high], 0)
+    real, imag = (
+        product(left[at : at + W], first) + product(left[2 * W + at : 3 * W + at], second)
+        for at in (0, W)
     )
     if conjugate:
-        return z[:W, :W] + z[W:, W:], z[:W, W:] - z[W:, :W]
-    return z[:W, :W] - z[W:, W:], z[:W, W:] + z[W:, :W]
+        return real[:, :W] + imag[:, W:], real[:, W:] - imag[:, :W]
+    return real[:, :W] - imag[:, W:], real[:, W:] + imag[:, :W]
 
 
 def at_window(meta, p, tile):
@@ -212,42 +225,63 @@
         out[chip, W : 2 * W, :] = field[1]
 
     def ahead(field, window):
-        return two_sided(*times(field, window), step_right[...], step_left[...], False)
-
-    def back(field, window):
-        return times_conjugate(window, two_sided(*field, step_right[...], step_left[...], True))
-
-    def forward_section(section, field):
+        return right_of(times(field, window), step_right[...], False)
+
+    def reached(y):
+        return left_of(y, step_left[...], False)
+
+    def back(y, window):
+        return times_conjugate(window, left_of(y, step_left[...], True))
+
+    def onward(field):
+        return right_of(field, step_right[...], True)
+
+    def forward_rest(section, y):
+        return lax.fori_loop(
+            1,
+            counts[section],
+            lambda slot, value: ahead(reached(value), rest_window(section, slot)),
+            y,
+        )
+
+    def forward_section(section, y):
+        field = reached(y)
+
         @pl.when((core == 0) & (section % 2 == 0))
         def _():
             keep(section // 2, field)
 
-        field = ahead(field, zero_window(section))
-        return lax.fori_loop(
-            1, counts[section], lambda slot, value: ahead(value, rest_window(section, slot)), field
-        )
-
-    def backward_section(index, field):
+        return forward_rest(section, ahead(field, zero_window(section)))
+
+    def backward_section(index, y):
         section = sections - 2 - index
-
-        @pl.when(section % 2 == 1)
+        count = counts[section]
+        y = lax.fori_loop(
+            1, count, lambda step, value: onward(back(value, rest_window(section, count - step))), y
+        )
+        field = back(y, zero_window(section))
+
+        @pl.when(section % 2 == 0)
         def _():
-            keep(section // 2, field)
-
-        count = counts[section]
-        field = lax.fori_loop(
-            1, count, lambda step, value: back(value, rest_window(section, count - step)), field
-        )
-        return back(field, zero_window(section))
+            keep(section // 2 - 1, field)
+
+        return onward(field)
 
     last = sections - 1
     final = counts[last] - 1
-    field = lax.fori_loop(0, last, forward_section, (illumination[0], illumination[1]))
-    field = lax.fori_loop(
-        0, final, lambda slot, value: ahead(value, any_window(last, slot)), field
+    start = illumination[0], illumination[1]
+
+    @pl.when(core == 0)
+    def _():
+        keep(0, start)
+
+    y = forward_rest(0, ahead(start, zero_window(0)))
+    y = lax.fori_loop(1, last, forward_section, y)
+    y = lax.fori_loop(
+        0, final, lambda slot, value: ahead(reached(value), any_window(last, slot)), y
     )
-    field = times(field, any_window(last, final))
-    real, imag = two_sided(*field, far_right[...], far_left[...], False)
+    field = times(reached(y), any_window(last, final))
+    real, imag = left_of(right_of(field, far_right[...], False), far_left[...], False)
     misfit = real * real + imag * imag - measured[meta[PLACE] // 2]
     loss = jnp.sum(misfit * misfit) * (1.0 / (W * W))
     for chip in range(chips):
@@ -255,15 +289,17 @@
 
     @pl.when(core == 1)
     def _():
-        spread = two_sided(
-            4.0 * misfit * real, 4.0 * misfit * imag, far_right[...], far_left[...], True
-        )
+        seed = 4.0 * misfit * real, 4.0 * misfit * imag
+        spread = left_of(right_of(seed, far_right[...], True), far_left[...], True)
         keep(chips - 1, spread)
-        value = times_conjugate(any_window(last, final), spread)
-        value = lax.fori_loop(
-            0, final, lambda step, value: back(value, any_window(last, final - 1 - step)), value
-        )
-        keep(0, lax.fori_loop(0, sections - 3, backward_section, value))
+        y = onward(times_conjugate(any_window(last, final), spread))
+        y = lax.fori_loop(
+            0,
+            final,
+            lambda step, value: onward(back(value, any_window(last, final - 1 - step))),
+            y,
+        )
+        lax.fori_loop(0, sections - 3, backward_section, y)
 
 
 GROUP = 4

time: 219 us -> 218 us (level)
  no operation moved by 1% of the time
where the time goes in v1:
time: 218 us
  blocking collectives  75.9 us (35%)
  starting transfers between devices  49.9 us (23%)
  waiting for transfers between devices  46.2 us (21%)
  Pallas kernels  39.7 us (18%)
  local copies, waits for them, and re-layouts  4.51 us (2%)
    all_to_all x1, blocking collectives, shards(): mine_rest = exchange(sent)  54.2 us
    ppermute x3, waiting for transfers between devices, moved(): lax.ppermute(block, axis, [((i - distance) % count, i) for i in range(cou...  35 us
    ppermute x3, starting transfers between devices, moved(): lax.ppermute(block, axis, [((i - distance) % count, i) for i in range(cou...  22.7 us
    all_to_all x1, blocking collectives, shards(): arrived = exchange(boundary)  21.7 us
    ppermute x3, starting transfers between devices, swapped(): return lax.ppermute(block, 'depth', [(i ^ 1, i) for i in range(count)])  19.4 us
    pallas_call x1, Pallas kernels, shards(): pl.pallas_call(wave_kernel, out_shape=jax.ShapeDtypeStruct((chips, 2 * W...  16.5 us
    pallas_call x1, Pallas kernels, shards(): pl.pallas_call(second_kernel, out_shape=(jax.ShapeDtypeStruct((slots, 2,...  10.3 us
    all_to_all x1, starting transfers between devices, shards(): mine_zero = exchange(zero)  7.68 us
  transfers between devices with their start and end apart: 7, of which 6 were waited for; matrix products, arithmetic and copies ran while one was open for 1% of the time, Pallas kernels for 1%

profile of v1, /device:TPU:8, one launch (start us, length us, event | category | flops | bytes accessed | tf_op | source)
XLA Modules:
  0.0 217.7 jit_solution(3800689286292748944)
XLA Ops:
  0.6 0.0 copy-start
  0.6 0.0 copy-start.11
  0.7 0.0 copy-start.10
  0.7 0.0 copy-start.9
  0.7 1.1 slice.7
  1.8 13.1 %collective-permute-start = (f32[1,2,256,128]{3,2,1,0:T(8,128)S(1)}, f32[1,2,256,128]{3,2,1,0:T(8,128)S(1)}, u32[]{:S(2)}, u32[]{:S(2)}) collective-permute-start(f32[1,2,256,128]{3,2,1,0:T(8,128)S(1)} %slice.7), channel_id=1, source_target_pairs={{1,0},{2,1},{3,2},{4,3},{5,4},{6,5},{7,6},{8,7},{9,8},{10,9},{11,1... | collective-permute-start | bytes 786440 | tf_op jit(solution)/shard_map/ppermute | solution.py:23
  14.9 1.9 slice.6
  17.4 0.0 copy-done.11
  17.5 0.0 copy-done.10
  17.5 0.0 copy-done.9
  17.5 0.1 concatenate.3.meta
  17.6 2.9 %collective-permute-done.rim = f32[1,2,256,128]{3,2,1,0:T(8,128)S(1)} collective-permute-done((f32[1,2,256,128]{3,2,1,0:T(8,128)S(1)}, f32[1,2,256,128]{3,2,1,0:T(8,128)S(1)}, u32[]{:S(2)}, u32[]{:S(2)}) %collective-permute-start) | collective-permute-done | bytes 262176 | tf_op jit(solution)/shard_map/ppermute | solution.py:23
  20.4 0.0 copy-done
  20.5 2.9 %cut.2.zero = f32[8,264,128]{2,1,0:T(8,128)} custom-call(s32[26]{0:T(128)S(1)} %concatenate.3.meta, f32[3,2,256,256]{3,2,1,0:T(8,128)S(1)} %copy-done, f32[1,2,256,128]{3,2,1,0:T(8,128)S(1)} %collective-permute-done.rim), custom_call_target="tpu_custom_call" | custom-call | tf_op jit(solution)/shard_map/cut/pallas_call | solution.py:496
  23.4 0.0 copy-start.8
  23.4 7.7 %all-to-all-start = ((f32[8,264,128]{2,1,0:T(8,128)}), f32[8,264,128]{2,1,0:T(8,128)S(1)}, u32[]{:S(2)}, u32[]{:S(2)}) async-start(f32[8,264,128]{2,1,0:T(8,128)} %cut.2.zero), calls=%async_computation | async-start | bytes 2162688 | tf_op jit(solution)/shard_map/all_to_all | solution.py:512
  31.0 0.0 copy-done.8
  31.0 7.7 %collective-permute-start.1 = (f32[2,2,256,128]{3,2,1,0:T(8,128)S(1)}, f32[2,2,256,128]{3,2,1,0:T(8,128)S(1)}, u32[]{:S(2)}, u32[]{:S(2)}) collective-permute-start(f32[2,2,256,128]{3,2,1,0:T(8,128)S(1)} %copy-done.8), channel_id=1, source_target_pairs={{1,0},{2,1},{3,2},{4,3},{5,4},{6,5},{7,6},{8,7},{9,8},{10,9},{11,1... | collective-permute-start | bytes 1572872 | tf_op jit(solution)/shard_map/ppermute | solution.py:23
  38.8 9.7 %collective-permute-done.1.rim = f32[2,2,256,128]{3,2,1,0:T(8,128)S(1)} collective-permute-done((f32[2,2,256,128]{3,2,1,0:T(8,128)S(1)}, f32[2,2,256,128]{3,2,1,0:T(8,128)S(1)}, u32[]{:S(2)}, u32[]{:S(2)}) %collective-permute-start.1) | collective-permute-done | bytes 524320 | tf_op jit(solution)/shard_map/ppermute | solution.py:23
  48.5 0.0 copy-start.1
  48.5 1.4 copy-done.1
  49.9 2.6 %cut.3.rest = f32[8,512,128]{2,1,0:T(8,128)S(1)} custom-call(s32[26]{0:T(128)S(1)} %concatenate.3.meta, f32[3,2,256,256]{3,2,1,0:T(8,128)S(1)} %copy-done.1, f32[2,2,256,128]{3,2,1,0:T(8,128)S(1)} %collective-permute-done.1.rim), custom_call_target="tpu_custom_call" | custom-call | tf_op jit(solution)/shard_map/cut/pallas_call | solution.py:496
  52.5 0.0 copy-start.2
  52.5 5.7 %all-to-all-done.mine_zero = f32[8,264,128]{2,1,0:T(8,128)S(1)} async-done(((f32[8,264,128]{2,1,0:T(8,128)}), f32[8,264,128]{2,1,0:T(8,128)S(1)}, u32[]{:S(2)}, u32[]{:S(2)}) %all-to-all-start) | async-done | bytes 1081376 | tf_op jit(solution)/shard_map/all_to_all | solution.py:512
  58.2 0.0 copy-start.3
  58.2 0.0 copy-start.4
  58.2 0.0 copy-start.5
  58.2 0.0 copy-start.6
  58.2 0.0 copy-start.7
  58.2 54.2 %all_to_all.15.mine_rest = f32[8,512,128]{2,1,0:T(8,128)S(1)} all-to-all(f32[8,512,128]{2,1,0:T(8,128)S(1)} %cut.3.rest), channel_id=1, replica_groups={{0,64,128,192,256,320,384,448},{32,96,160,224,288,352,416,480},{1,65,12..., dimensions={0} | all-to-all | bytes 4194304 | tf_op jit(solution)/shard_map/all_to_all | solution.py:516
  112.4 1.9 collective-permute-start.3
  114.3 2.4 %collective-permute-start.2 = (f32[8,264,128]{2,1,0:T(8,128)S(1)}, f32[8,264,128]{2,1,0:T(8,128)S(1)}, u32[]{:S(2)}, u32[]{:S(2)}) collective-permute-start(f32[8,264,128]{2,1,0:T(8,128)S(1)} %all-to-all-done.mine_zero), channel_id=1, source_target_pairs={{32,0},{0,32},{96,64},{64,96},{160,128},{128,160},{224,192},{192,2... | collective-permute-start | bytes 3244040 | tf_op jit(solution)/shard_map/ppermute | solution.py:28
  116.8 3.3 %collective-permute-done.2.other_zero = f32[8,264,128]{2,1,0:T(8,128)S(1)} collective-permute-done((f32[8,264,128]{2,1,0:T(8,128)S(1)}, f32[8,264,128]{2,1,0:T(8,128)S(1)}, u32[]{:S(2)}, u32[]{:S(2)}) %collective-permute-start.2) | collective-permute-done | bytes 1081376 | tf_op jit(solution)/shard_map/ppermute | solution.py:28
  120.0 0.0 collective-permute-done.3.other_rest
  120.0 0.0 copy-done.2
  120.0 0.0 copy-done.3
  120.0 0.0 copy-done.4
  120.0 0.0 copy-done.5
  120.0 0.0 copy-done.6
  120.1 0.0 copy-done.7
  120.1 16.5 %wave.1 = f32[8,264,128]{2,1,0:T(8,128)S(1)} custom-call(s32[26]{0:T(128)S(1)} %concatenate.3.meta, f32[8,264,128]{2,1,0:T(8,128)S(1)} %all-to-all-done.mine_zero, f32[8,264,128]{2,1,0:T(8,128)S(1)} %collective-permute-done.2.other_zero, f32[8,512,128]{2,1,0:T(8,128)S(1)} %all_to_all.15.mine_rest, f32[8,512,128]{2,1,0:T(8,128)S(1)} %collective-permute-done.3.other_rest, ...), custom_call_target="tpu_custom_call" | custom-call | tf_op jit(solution)/shard_map/wave/pallas_call | solution.py:518
  136.5 21.7 %all_to_all.16.arrived = f32[8,264,128]{2,1,0:T(8,128)S(1)} all-to-all(f32[8,264,128]{2,1,0:T(8,128)S(1)} %wave.1), channel_id=1, replica_groups={{0,64,128,192,256,320,384,448},{32,96,160,224,288,352,416,480},{1,65,12..., dimensions={0} | all-to-all | bytes 2162688 | tf_op jit(solution)/shard_map/all_to_all | solution.py:527
  158.2 6.2 %first.1 = (f32[8,768,128]{2,1,0:T(8,128)S(1)}, f32[8,256,128]{2,1,0:T(8,128)S(1)}) custom-call(s32[26]{0:T(128)S(1)} %concatenate.3.meta, f32[8,264,128]{2,1,0:T(8,128)} %cut.2.zero, f32[8,512,128]{2,1,0:T(8,128)S(1)} %cut.3.rest, f32[8,264,128]{2,1,0:T(8,128)S(1)} %all_to_all.16.arrived, bf16[512,256]{1,0:T(8,128)(2,1)S(1)} %copy-done.3, ...), custom_call_target="tpu_custom_call" | custom-call | tf_op jit(solution)/shard_map/first/pallas_call | solution.py:528
  164.4 15.1 %collective-permute-start.4 = (f32[8,256,128]{2,1,0:T(8,128)S(1)}, f32[8,256,128]{2,1,0:T(8,128)S(1)}, u32[]{:S(2)}, u32[]{:S(2)}) collective-permute-start(f32[8,256,128]{2,1,0:T(8,128)S(1)} %get-tuple-element.14), channel_id=1, source_target_pairs={{32,0},{0,32},{96,64},{64,96},{160,128},{128,160},{224,192},{192,2... | collective-permute-start | bytes 3145736 | tf_op jit(solution)/shard_map/ppermute | solution.py:28
  179.5 2.3 %collective-permute-done.4.handed = f32[8,256,128]{2,1,0:T(8,128)S(1)} collective-permute-done((f32[8,256,128]{2,1,0:T(8,128)S(1)}, f32[8,256,128]{2,1,0:T(8,128)S(1)}, u32[]{:S(2)}, u32[]{:S(2)}) %collective-permute-start.4) | collective-permute-done | bytes 1048608 | tf_op jit(solution)/shard_map/ppermute | solution.py:28
  181.8 10.3 %second.1 = (f32[3,2,256,256]{3,2,1,0:T(8,128)S(1)}, f32[3,2,256,128]{3,2,1,0:T(8,128)S(1)}, f32[1,8]{1,0:T(1,128)}) custom-call(s32[26]{0:T(128)S(1)} %concatenate.3.meta, f32[8,264,128]{2,1,0:T(8,128)} %cut.2.zero, f32[8,512,128]{2,1,0:T(8,128)S(1)} %cut.3.rest, f32[8,768,128]{2,1,0:T(8,128)S(1)} %get-tuple-element.13.track, ...), custom_call_target="tpu_custom_call" | custom-call | tf_op jit(solution)/shard_map/second/pallas_call | solution.py:539
  192.1 1.9 collective-permute-start.5
  194.0 22.4 %collective-permute-done.5.rim = f32[3,2,256,128]{3,2,1,0:T(8,128)S(1)} collective-permute-done((f32[3,2,256,128]{3,2,1,0:T(8,128)S(1)}, f32[3,2,256,128]{3,2,1,0:T(8,128)S(1)}, u32[]{:S(2)}, u32[]{:S(2)}) %collective-permute-start.5) | collective-permute-done | bytes 786464 | tf_op jit(solution)/shard_map/ppermute | solution.py:23
  216.4 1.3 merge.1
Async XLA Ops:
  0.6 19.8 %copy-start = (f32[3,2,256,256]{3,2,1,0:T(8,128)S(1)}, f32[3,2,256,256]{3,2,1,0:T(8,128)}, u32[]{:S(2)}) copy-start(f32[3,2,256,256]{3,2,1,0:T(8,128)} %own.3) | copy-start | bytes 4718596
  0.6 16.8 %copy-start.11 = (s32[1,8]{1,0:T(1,128)S(1)}, s32[1,8]{1,0:T(1,128)}, u32[]{:S(2)}) copy-start(s32[1,8]{1,0:T(1,128)} %param.15) | copy-start | bytes 100
  0.7 16.8 %copy-start.10 = (s32[8]{0:T(128)S(1)}, s32[8]{0:T(128)}, u32[]{:S(2)}) copy-start(s32[8]{0:T(128)} %param.14) | copy-start | bytes 100
  0.7 16.8 %copy-start.9 = (s32[8]{0:T(128)S(1)}, s32[8]{0:T(128)}, u32[]{:S(2)}) copy-start(s32[8]{0:T(128)} %param.13) | copy-start | bytes 100
  1.8 18.7 %collective-permute-start = (f32[1,2,256,128]{3,2,1,0:T(8,128)S(1)}, f32[1,2,256,128]{3,2,1,0:T(8,128)S(1)}, u32[]{:S(2)}, u32[]{:S(2)}) collective-permute-start(f32[1,2,256,128]{3,2,1,0:T(8,128)S(1)} %slice.7), channel_id=1, source_target_pairs={{1,0},{2,1},{3,2},{4,3},{5,4},{6,5},{7,6},{8,7},{9,8},{10,9},{11,1... | collective-permute-start | bytes 786440 | tf_op jit(solution)/shard_map/ppermute | solution.py:23
  23.4 7.7 %copy-start.8 = (f32[2,2,256,128]{3,2,1,0:T(8,128)S(1)}, f32[2,2,256,128]{3,2,1,0:T(8,128)}, u32[]{:S(2)}) copy-start(f32[2,2,256,128]{3,2,1,0:T(8,128)} %slice.6) | copy-start | bytes 1572868
  23.4 34.8 %all-to-all-start = ((f32[8,264,128]{2,1,0:T(8,128)}), f32[8,264,128]{2,1,0:T(8,128)S(1)}, u32[]{:S(2)}, u32[]{:S(2)}) async-start(f32[8,264,128]{2,1,0:T(8,128)} %cut.2.zero), calls=%async_computation | async-start | bytes 2162688 | tf_op jit(solution)/shard_map/all_to_all | solution.py:512
  31.0 17.5 %collective-permute-start.1 = (f32[2,2,256,128]{3,2,1,0:T(8,128)S(1)}, f32[2,2,256,128]{3,2,1,0:T(8,128)S(1)}, u32[]{:S(2)}, u32[]{:S(2)}) collective-permute-start(f32[2,2,256,128]{3,2,1,0:T(8,128)S(1)} %copy-done.8), channel_id=1, source_target_pairs={{1,0},{2,1},{3,2},{4,3},{5,4},{6,5},{7,6},{8,7},{9,8},{10,9},{11,1... | collective-permute-start | bytes 1572872 | tf_op jit(solution)/shard_map/ppermute | solution.py:23
  48.5 1.4 copy-start.1
  52.5 67.6 %copy-start.2 = (bf16[512,256]{1,0:T(8,128)(2,1)S(1)}, bf16[512,256]{1,0:T(8,128)(2,1)}, u32[]{:S(2)}) copy-start(bf16[512,256]{1,0:T(8,128)(2,1)} %constant.15.clone.step_left) | copy-start | bytes 786436
  58.2 61.9 %copy-start.3 = (bf16[512,256]{1,0:T(8,128)(2,1)S(1)}, bf16[512,256]{1,0:T(8,128)(2,1)}, u32[]{:S(2)}) copy-start(bf16[512,256]{1,0:T(8,128)(2,1)} %constant.14.clone.step_right) | copy-start | bytes 786436
  58.2 61.9 %copy-start.4 = (f32[8,128,128]{2,1,0:T(8,128)S(1)}, f32[8,128,128]{2,1,0:T(8,128)}, u32[]{:S(2)}) copy-start(f32[8,128,128]{2,1,0:T(8,128)} %measured.1) | copy-start | bytes 1572868
  58.2 61.9 %copy-start.5 = (bf16[512,256]{1,0:T(8,128)(2,1)S(1)}, bf16[512,256]{1,0:T(8,128)(2,1)}, u32[]{:S(2)}) copy-start(bf16[512,256]{1,0:T(8,128)(2,1)} %constant.17.clone.far_left) | copy-start | bytes 786436
  58.2 61.9 %copy-start.6 = (bf16[512,256]{1,0:T(8,128)(2,1)S(1)}, bf16[512,256]{1,0:T(8,128)(2,1)}, u32[]{:S(2)}) copy-start(bf16[512,256]{1,0:T(8,128)(2,1)} %constant.16.clone.far_right) | copy-start | bytes 786436
  58.2 61.9 %copy-start.7 = (f32[2,128,128]{2,1,0:T(8,128)S(1)}, f32[2,128,128]{2,1,0:T(8,128)}, u32[]{:S(2)}) copy-start(f32[2,128,128]{2,1,0:T(8,128)} %illumination.1) | copy-start | bytes 393220
  112.4 7.6 %collective-permute-start.3 = (f32[8,512,128]{2,1,0:T(8,128)S(1)}, f32[8,512,128]{2,1,0:T(8,128)S(1)}, u32[]{:S(2)}, u32[]{:S(2)}) collective-permute-start(f32[8,512,128]{2,1,0:T(8,128)S(1)} %all_to_all.15.mine_rest), channel_id=1, source_target_pairs={{32,0},{0,32},{96,64},{64,96},{160,128},{128,160},{224,192},{192,2... | collective-permute-start | bytes 6291464 | tf_op jit(solution)/shard_map/ppermute | solution.py:28
  114.3 5.7 %collective-permute-start.2 = (f32[8,264,128]{2,1,0:T(8,128)S(1)}, f32[8,264,128]{2,1,0:T(8,128)S(1)}, u32[]{:S(2)}, u32[]{:S(2)}) collective-permute-start(f32[8,264,128]{2,1,0:T(8,128)S(1)} %all-to-all-done.mine_zero), channel_id=1, source_target_pairs={{32,0},{0,32},{96,64},{64,96},{160,128},{128,160},{224,192},{192,2... | collective-permute-start | bytes 3244040 | tf_op jit(solution)/shard_map/ppermute | solution.py:28
  164.4 17.4 %collective-permute-start.4 = (f32[8,256,128]{2,1,0:T(8,128)S(1)}, f32[8,256,128]{2,1,0:T(8,128)S(1)}, u32[]{:S(2)}, u32[]{:S(2)}) collective-permute-start(f32[8,256,128]{2,1,0:T(8,128)S(1)} %get-tuple-element.14), channel_id=1, source_target_pairs={{32,0},{0,32},{96,64},{64,96},{160,128},{128,160},{224,192},{192,2... | collective-permute-start | bytes 3145736 | tf_op jit(solution)/shard_map/ppermute | solution.py:28
  192.1 24.3 %collective-permute-start.5 = (f32[3,2,256,128]{3,2,1,0:T(8,128)S(1)}, f32[3,2,256,128]{3,2,1,0:T(8,128)S(1)}, u32[]{:S(2)}, u32[]{:S(2)}) collective-permute-start(f32[3,2,256,128]{3,2,1,0:T(8,128)S(1)} %get-tuple-element.16), channel_id=1, source_target_pairs={{31,0},{0,1},{1,2},{2,3},{3,4},{4,5},{5,6},{6,7},{7,8},{8,9},{9,10... | collective-permute-start | bytes 2359304 | tf_op jit(solution)/shard_map/ppermute | solution.py:23
